TPU v7x, 128 devices: a whole 4x4x4 slice. The times are simulated.
128 devices in a mesh: seg: 16 (over z, y_lo, core), section: 8 (over y_hi, x).
Axes of the slice: x: 4, y: 4 (y_hi: 2, y_lo: 2; y = y_hi * 2 + y_lo), z: 4, core: 2. Of those that a mesh axis runs over, the one named last changes fastest.
Arguments:
- leaving: bfloat16 [16, 8, 272, 4096], P('seg', 'section'), may hold values from -6 to 6
- w_query: bfloat16 [8, 4096, 2048], P('section'), may hold values from -0.09375 to 0.09375
- w_key: bfloat16 [8, 4096, 2048], P('section', None, 'seg'), may hold values from -0.09375 to 0.09375
- w_value: bfloat16 [8, 4096, 4096], P('section', None, 'seg'), may hold values from -0.09375 to 0.09375
- w_gate: bfloat16 [8, 4096], P('section'), may hold values from -0.09375 to 0.09375
- norm_gain: bfloat16 [8, 4096], P('section'), may hold values from 0.5 to 1.5
- memory_matrix: bfloat16 [8, 4096, 2048], P('section', 'seg'), may hold values from -24 to 24
- key_totals: float32 [8, 2048], P('section'), may hold values from 0.02 to 0.5
- doc_starts: int32 [8, 16], P('section'), may hold values 0 or 1
Outputs:
- updated: bfloat16 [16, 8, 272, 4096], P('seg', 'section')
- matrix_next: bfloat16 [8, 4096, 2048], P('section', 'seg')
- totals_next: float32 [8, 2048], P('section')
All inputs are finite; a program needn't handle non-finite values. No bound on the sum of `doc_starts` on one device may be relied on, other than what follows from the above.
Results may differ from a plain program's by a relative error of at most 0.01.
Values may be sent and summed in bfloat16 or wider, within the bound.
No kernel may reach another device: no remote copies, remote signals or barrier semaphores. Data moves between devices by JAX's collectives and lax.ppermute only.
A program may use at most 128 MiB of HBM per device.

v0:
```python
import jax
import jax.numpy as jnp
from jax import lax
from jax.sharding import PartitionSpec as P

MEM = 16
highest = lax.Precision.HIGHEST
epsilon = 1e-05


def shifted(shard, axis, by):
    size = lax.axis_size(axis)
    return lax.ppermute(shard, axis, [(i, (i + by) % size) for i in range(size)])


def from_root(block, axis, source):
    block = jnp.where(lax.axis_index(axis) == source, block, jnp.zeros_like(block))
    return lax.psum(block, axis)


def feature_map(projected):
    return jax.nn.elu(projected) + 1.0


def contract_last(left_rows, right_rows):
    return lax.dot_general(
        left_rows, right_rows, (((1,), (1,)), ((), ())), preferred_element_type=jnp.float32
    )


def contract_first(left_rows, right_rows):
    return lax.dot_general(
        left_rows,
        right_rows,
        (((0,), (0,)), ((), ())),
        precision=highest,
        preferred_element_type=jnp.float32,
    )


def visibility(starts_row):
    seg_total = starts_row.shape[0]
    positions = jnp.arange(seg_total, dtype=jnp.int32)
    last_start = lax.cummax(jnp.where(starts_row == 1, positions, jnp.int32(-1)), axis=0)
    fresh_flag = (last_start < 0).astype(jnp.float32)
    seen_pairs = (
        (positions[:, None] >= last_start[None, :]) & (positions[:, None] < positions[None, :])
    ).astype(jnp.float32)
    seen_final = (positions >= last_start[seg_total - 1]).astype(jnp.float32)
    return (fresh_flag, seen_pairs, seen_final)


def local(
    leaving, w_query, w_key, w_value, w_gate, norm_gain, memory_matrix, key_totals, doc_starts
):
    entering = shifted(leaving, "section", 1)[0, 0]
    row_count = entering.shape[0]
    feature_count = entering.shape[1]
    seg_count = lax.axis_size("seg")
    my_index = lax.axis_index("seg")
    wide_rows = entering.astype(jnp.float32)
    inverse_rms = lax.rsqrt(jnp.mean(wide_rows * wide_rows, axis=-1, keepdims=True) + epsilon)
    normed = (wide_rows * inverse_rms * norm_gain[0].astype(jnp.float32)).astype(jnp.bfloat16)
    queries = feature_map(jnp.dot(normed, w_query[0], preferred_element_type=jnp.float32)).astype(
        jnp.bfloat16
    )
    memory = lax.all_gather(normed[:MEM], "seg", axis=0, tiled=True)
    key_part = feature_map(jnp.dot(memory, w_key[0], preferred_element_type=jnp.float32)).astype(
        jnp.bfloat16
    )
    value_part = jnp.dot(memory, w_value[0], preferred_element_type=jnp.float32)
    gate_rates = jax.nn.sigmoid(jnp.dot(memory, w_gate[0], preferred_element_type=jnp.float32))
    key_rows = lax.all_gather(key_part, "seg", axis=1, tiled=True)
    values = lax.all_to_all(
        value_part.reshape(seg_count, MEM, value_part.shape[1]).astype(jnp.bfloat16),
        "seg",
        split_axis=0,
        concat_axis=2,
        tiled=True,
    ).astype(jnp.float32)[0]
    fresh_flag, seen_pairs, seen_final = visibility(doc_starts[0])
    key_wide = key_rows.astype(jnp.float32)
    key_sums = key_wide.reshape(seg_count, MEM, -1).sum(axis=1)
    totals = fresh_flag[:, None] * key_totals[0][None, :] + jnp.dot(
        seen_pairs.T, key_sums, precision=highest
    )
    total_rows = jnp.repeat(totals, MEM, axis=0)
    key_scales = jnp.maximum(jnp.sum(total_rows * key_wide, axis=-1), 1.0)
    key_gram = contract_last(key_rows, key_rows)
    seen_cols = jnp.repeat(jnp.repeat(seen_pairs, MEM, axis=0), MEM, axis=1)
    mixing = seen_cols * key_gram * (gate_rates / key_scales)[None, :]
    my_keys = lax.dynamic_slice_in_dim(key_rows, my_index * MEM, MEM, 0)
    probes = jnp.concatenate([queries, my_keys], axis=0)
    probed_all = contract_last(probes, lax.all_gather(memory_matrix[0], "seg", axis=0, tiled=True))
    base_read = probed_all[:row_count]
    probed_keys = probed_all[row_count:]
    my_fresh = fresh_flag[my_index]
    my_rates = lax.dynamic_slice_in_dim(gate_rates, my_index * MEM, MEM, 0)
    my_scales = lax.dynamic_slice_in_dim(key_scales, my_index * MEM, MEM, 0)
    initial = my_rates[:, None] * (values - my_fresh * probed_keys / my_scales[:, None])
    writes = jnp.zeros((seg_count * MEM, feature_count), jnp.float32)

    def relay_step(step_index, current):
        mix_cols = lax.dynamic_slice_in_dim(mixing, step_index * MEM, MEM, 1)
        candidate = initial - contract_first(mix_cols, current)
        arrived = from_root(candidate.astype(jnp.bfloat16), "seg", step_index).astype(
            candidate.dtype
        )
        return lax.dynamic_update_slice_in_dim(current, arrived, step_index * MEM, 0)

    writes = lax.fori_loop(0, seg_count, relay_step, writes)
    column_mask = jnp.repeat(seen_pairs[:, my_index], MEM)
    similarity = contract_last(queries, key_rows) * column_mask[None, :]
    low_rank = jnp.dot(similarity, writes, precision=highest)
    my_totals = lax.dynamic_slice_in_dim(totals, my_index, 1, 0)
    denominator = jnp.maximum(jnp.sum(queries.astype(jnp.float32) * my_totals, axis=-1), 1.0)
    updated = (wide_rows + (my_fresh * base_read + low_rank) / denominator[:, None]).astype(
        jnp.bfloat16
    )
    slab_width = memory_matrix.shape[1]
    write_cols = lax.dynamic_slice_in_dim(writes, my_index * slab_width, slab_width, 1)
    end_rows = jnp.repeat(seen_final, MEM)
    fresh_end = fresh_flag[seg_count - 1]
    matrix_next = (
        fresh_end * memory_matrix[0].astype(jnp.float32)
        + contract_first(write_cols * end_rows[:, None], key_wide)
    ).astype(jnp.bfloat16)
    totals_next = fresh_end * key_totals[0] + jnp.dot(seen_final, key_sums, precision=highest)
    return (updated[None, None], matrix_next[None], totals_next[None])


def solution(mesh):
    return jax.shard_map(
        local,
        mesh=mesh,
        in_specs=(
            P("seg", "section", None, None),
            P("section", None, None),
            P("section", None, "seg"),
            P("section", None, "seg"),
            P("section", None),
            P("section", None),
            P("section", "seg", None),
            P("section", None),
            P("section", None),
        ),
        out_specs=(P("seg", "section", None, None), P("section", "seg", None), P("section", None)),
        check_vma=False,
    )
```

profile of v0, /device:TPU:1, one launch (start us, length us, event | category | flops | bytes accessed | tf_op | source)
XLA Modules:
  0.0 2270.6 jit_solution(1127673724252390452)
XLA Ops:
  10.1 51.4 %collective-permute-done = bf16[1,1,272,4096]{3,2,1,0:T(8,128)(2,1)S(1)} collective-permute-done((bf16[1,1,272,4096]{3,2,1,0:T(8,128)(2,1)}, bf16[1,1,272,4096]{3,2,1,0:T(8,128)(2,1)S(1)}, u32[]{:S(2)}, u32[]{:S(2)}) %collective-permute-start) | collective-permute-done | bytes 2228256 | tf_op jit(solution)/shard_map/ppermute | solution.py:13
  63.6 35.1 %all-gather.5.cloned.1.call-done = bf16[256,4096]{1,0:T(8,128)(2,1)} async-done(((bf16[16,4096]{1,0:T(8,128)(2,1)}), bf16[256,4096]{1,0:T(8,128)(2,1)}) %all-gather.5.cloned.1.call-update) | async-done | bytes 2097168 | tf_op jit(solution)/shard_map/all_gather | solution.py:67
  119.6 16.4 all-gather.7.cloned.1.call-done
  139.8 9.8 multiply_reduce_fusion.1
  154.0 75.3 %all-gather.9.cloned.1.call-done = bf16[1,4096,2048]{2,1,0:T(8,128)(2,1)} async-done(((bf16[1,256,2048]{2,1,0:T(8,128)(2,1)}), bf16[1,4096,2048]{2,1,0:T(8,128)(2,1)}) %all-gather.9.cloned.1.call-update) | async-done | bytes 16777232 | tf_op jit(solution)/shard_map/all_gather | solution.py:94
  229.4 9.0 fusion.4
  241.8 2007.7 %while.13 = (s32[]{:T(128)}, f32[256,4096]{1,0:T(8,128)}, f32[256,256]{1,0:T(8,128)}, f32[16,4096]{1,0:T(8,128)S(1)}, s32[]{:T(128)}, /*index=5*/s32[]{:T(128)}, s32[]{:T(128)}, s32[]{:T(128)}, u32[]{:T(128)}, u32[]{:T(128)}) while((s32[]{:T(128)}, f32[256,4096]{1,0:T(8,128)}, f32[256,256]{1,0:T(8,128)}, f32[16,4096]{1,0:T(8,128)S(1)}, ...), condition=%wide.region_6.7_spmd, body=%wide.region_4.6_spmd.sunk | while | flops 201654288 | bytes 5898477 | solution.py:111
  246.8 118.6 %all-reduce.2.cloned.1.call-done = bf16[16,4096]{1,0:T(8,128)(2,1)} async-done(((bf16[16,4096]{1,0:T(8,128)(2,1)}), bf16[16,4096]{1,0:T(8,128)(2,1)}) %all-reduce.2.cloned.1.call-update) | async-done | bytes 131088 | tf_op jit(solution)/shard_map/while/body/eval_jaxpr/psum | solution.py:18
  372.1 118.8 %all-reduce.2.cloned.1.call-done = bf16[16,4096]{1,0:T(8,128)(2,1)} async-done(((bf16[16,4096]{1,0:T(8,128)(2,1)}), bf16[16,4096]{1,0:T(8,128)(2,1)}) %all-reduce.2.cloned.1.call-update) | async-done | bytes 131088 | tf_op jit(solution)/shard_map/while/body/eval_jaxpr/psum | solution.py:18
  497.6 118.8 %all-reduce.2.cloned.1.call-done = bf16[16,4096]{1,0:T(8,128)(2,1)} async-done(((bf16[16,4096]{1,0:T(8,128)(2,1)}), bf16[16,4096]{1,0:T(8,128)(2,1)}) %all-reduce.2.cloned.1.call-update) | async-done | bytes 131088 | tf_op jit(solution)/shard_map/while/body/eval_jaxpr/psum | solution.py:18
  623.1 118.8 %all-reduce.2.cloned.1.call-done = bf16[16,4096]{1,0:T(8,128)(2,1)} async-done(((bf16[16,4096]{1,0:T(8,128)(2,1)}), bf16[16,4096]{1,0:T(8,128)(2,1)}) %all-reduce.2.cloned.1.call-update) | async-done | bytes 131088 | tf_op jit(solution)/shard_map/while/body/eval_jaxpr/psum | solution.py:18
  748.6 118.8 %all-reduce.2.cloned.1.call-done = bf16[16,4096]{1,0:T(8,128)(2,1)} async-done(((bf16[16,4096]{1,0:T(8,128)(2,1)}), bf16[16,4096]{1,0:T(8,128)(2,1)}) %all-reduce.2.cloned.1.call-update) | async-done | bytes 131088 | tf_op jit(solution)/shard_map/while/body/eval_jaxpr/psum | solution.py:18
  874.1 118.8 %all-reduce.2.cloned.1.call-done = bf16[16,4096]{1,0:T(8,128)(2,1)} async-done(((bf16[16,4096]{1,0:T(8,128)(2,1)}), bf16[16,4096]{1,0:T(8,128)(2,1)}) %all-reduce.2.cloned.1.call-update) | async-done | bytes 131088 | tf_op jit(solution)/shard_map/while/body/eval_jaxpr/psum | solution.py:18
  999.6 118.8 %all-reduce.2.cloned.1.call-done = bf16[16,4096]{1,0:T(8,128)(2,1)} async-done(((bf16[16,4096]{1,0:T(8,128)(2,1)}), bf16[16,4096]{1,0:T(8,128)(2,1)}) %all-reduce.2.cloned.1.call-update) | async-done | bytes 131088 | tf_op jit(solution)/shard_map/while/body/eval_jaxpr/psum | solution.py:18
  1125.1 118.8 %all-reduce.2.cloned.1.call-done = bf16[16,4096]{1,0:T(8,128)(2,1)} async-done(((bf16[16,4096]{1,0:T(8,128)(2,1)}), bf16[16,4096]{1,0:T(8,128)(2,1)}) %all-reduce.2.cloned.1.call-update) | async-done | bytes 131088 | tf_op jit(solution)/shard_map/while/body/eval_jaxpr/psum | solution.py:18
  1250.6 118.8 %all-reduce.2.cloned.1.call-done = bf16[16,4096]{1,0:T(8,128)(2,1)} async-done(((bf16[16,4096]{1,0:T(8,128)(2,1)}), bf16[16,4096]{1,0:T(8,128)(2,1)}) %all-reduce.2.cloned.1.call-update) | async-done | bytes 131088 | tf_op jit(solution)/shard_map/while/body/eval_jaxpr/psum | solution.py:18
  1376.1 118.8 %all-reduce.2.cloned.1.call-done = bf16[16,4096]{1,0:T(8,128)(2,1)} async-done(((bf16[16,4096]{1,0:T(8,128)(2,1)}), bf16[16,4096]{1,0:T(8,128)(2,1)}) %all-reduce.2.cloned.1.call-update) | async-done | bytes 131088 | tf_op jit(solution)/shard_map/while/body/eval_jaxpr/psum | solution.py:18
  1501.6 118.8 %all-reduce.2.cloned.1.call-done = bf16[16,4096]{1,0:T(8,128)(2,1)} async-done(((bf16[16,4096]{1,0:T(8,128)(2,1)}), bf16[16,4096]{1,0:T(8,128)(2,1)}) %all-reduce.2.cloned.1.call-update) | async-done | bytes 131088 | tf_op jit(solution)/shard_map/while/body/eval_jaxpr/psum | solution.py:18
  1627.0 118.8 %all-reduce.2.cloned.1.call-done = bf16[16,4096]{1,0:T(8,128)(2,1)} async-done(((bf16[16,4096]{1,0:T(8,128)(2,1)}), bf16[16,4096]{1,0:T(8,128)(2,1)}) %all-reduce.2.cloned.1.call-update) | async-done | bytes 131088 | tf_op jit(solution)/shard_map/while/body/eval_jaxpr/psum | solution.py:18
  1752.5 118.8 %all-reduce.2.cloned.1.call-done = bf16[16,4096]{1,0:T(8,128)(2,1)} async-done(((bf16[16,4096]{1,0:T(8,128)(2,1)}), bf16[16,4096]{1,0:T(8,128)(2,1)}) %all-reduce.2.cloned.1.call-update) | async-done | bytes 131088 | tf_op jit(solution)/shard_map/while/body/eval_jaxpr/psum | solution.py:18
  1878.0 118.8 %all-reduce.2.cloned.1.call-done = bf16[16,4096]{1,0:T(8,128)(2,1)} async-done(((bf16[16,4096]{1,0:T(8,128)(2,1)}), bf16[16,4096]{1,0:T(8,128)(2,1)}) %all-reduce.2.cloned.1.call-update) | async-done | bytes 131088 | tf_op jit(solution)/shard_map/while/body/eval_jaxpr/psum | solution.py:18
  2003.5 118.8 %all-reduce.2.cloned.1.call-done = bf16[16,4096]{1,0:T(8,128)(2,1)} async-done(((bf16[16,4096]{1,0:T(8,128)(2,1)}), bf16[16,4096]{1,0:T(8,128)(2,1)}) %all-reduce.2.cloned.1.call-update) | async-done | bytes 131088 | tf_op jit(solution)/shard_map/while/body/eval_jaxpr/psum | solution.py:18
  2129.1 118.8 %all-reduce.2.cloned.1.call-done = bf16[16,4096]{1,0:T(8,128)(2,1)} async-done(((bf16[16,4096]{1,0:T(8,128)(2,1)}), bf16[16,4096]{1,0:T(8,128)(2,1)}) %all-reduce.2.cloned.1.call-update) | async-done | bytes 131088 | tf_op jit(solution)/shard_map/while/body/eval_jaxpr/psum | solution.py:18
  2253.7 10.3 fusion.11
  (144 shorter events, 148.6 us)
Async XLA Ops:
  7.2 98.1 %copy-start = (bf16[1,4096,256]{2,1,0:T(8,128)(2,1)S(1)}, bf16[1,4096,256]{2,1,0:T(8,128)(2,1)}, u32[]{:S(2)}) copy-start(bf16[1,4096,256]{2,1,0:T(8,128)(2,1)} %param.14) | copy-start | bytes 6291460
  7.2 91.5 %all-gather.5.cloned.1.call-start = ((), (), s32[]{:S(2)}) async-start(), calls=%async_computation.1 | async-start | bytes 2228224 | tf_op jit(solution)/shard_map/all_gather | solution.py:67
  7.2 54.2 %collective-permute-start = (bf16[1,1,272,4096]{3,2,1,0:T(8,128)(2,1)}, bf16[1,1,272,4096]{3,2,1,0:T(8,128)(2,1)S(1)}, u32[]{:S(2)}, u32[]{:S(2)}) collective-permute-start(bf16[1,1,272,4096]{3,2,1,0:T(8,128)(2,1)} %param.11), channel_id=1, source_target_pairs={{0,1},{1,2},{2,3},{3,4},{4,5},{5,6},{6,7},{7,0},{8,9},{9,10},{10,1... | collective-permute-start | bytes 6684680 | tf_op jit(solution)/shard_map/ppermute | solution.py:13
  62.0 36.7 %copy-start.6 = (bf16[1,4096,128]{2,1,0:T(8,128)(2,1)S(1)}, bf16[1,4096,128]{2,1,0:T(8,128)(2,1)}, u32[]{:S(2)}) copy-start(bf16[1,4096,128]{2,1,0:T(8,128)(2,1)} %param.13) | copy-start | bytes 3145732
  63.6 38.8 %copy-start.12 = (s32[1,16]{1,0:T(1,128)S(1)}, s32[1,16]{1,0:T(1,128)}, u32[]{:S(2)}) copy-start(s32[1,16]{1,0:T(1,128)} %param.19) | copy-start | bytes 196
  63.6 72.5 %all-gather.7.cloned.1.call-start = ((), (), s32[]{:S(2)}) async-start(), calls=%async_computation.2 | async-start | bytes 1114112 | tf_op jit(solution)/shard_map/all_gather | solution.py:73
  101.6 127.7 %all-gather.9.cloned.1.call-start = ((), (), s32[]{:S(2)}) async-start(), calls=%async_computation.3 | async-start | bytes 17825792 | tf_op jit(solution)/shard_map/all_gather | solution.py:94
  108.2 10.6 all-to-all-start
  241.8 123.7 %all-reduce.2.cloned.1.call-start = ((), (), s32[]{:S(2)}) async-start(), calls=%async_computation.4 | async-start | bytes 262144 | tf_op jit(solution)/shard_map/while/body/eval_jaxpr/psum | solution.py:18
  367.1 123.9 %all-reduce.2.cloned.1.call-start = ((), (), s32[]{:S(2)}) async-start(), calls=%async_computation.4 | async-start | bytes 262144 | tf_op jit(solution)/shard_map/while/body/eval_jaxpr/psum | solution.py:18
  492.5 123.9 %all-reduce.2.cloned.1.call-start = ((), (), s32[]{:S(2)}) async-start(), calls=%async_computation.4 | async-start | bytes 262144 | tf_op jit(solution)/shard_map/while/body/eval_jaxpr/psum | solution.py:18
  618.0 123.9 %all-reduce.2.cloned.1.call-start = ((), (), s32[]{:S(2)}) async-start(), calls=%async_computation.4 | async-start | bytes 262144 | tf_op jit(solution)/shard_map/while/body/eval_jaxpr/psum | solution.py:18
  743.5 123.9 %all-reduce.2.cloned.1.call-start = ((), (), s32[]{:S(2)}) async-start(), calls=%async_computation.4 | async-start | bytes 262144 | tf_op jit(solution)/shard_map/while/body/eval_jaxpr/psum | solution.py:18
  869.0 123.9 %all-reduce.2.cloned.1.call-start = ((), (), s32[]{:S(2)}) async-start(), calls=%async_computation.4 | async-start | bytes 262144 | tf_op jit(solution)/shard_map/while/body/eval_jaxpr/psum | solution.py:18
  994.5 123.9 %all-reduce.2.cloned.1.call-start = ((), (), s32[]{:S(2)}) async-start(), calls=%async_computation.4 | async-start | bytes 262144 | tf_op jit(solution)/shard_map/while/body/eval_jaxpr/psum | solution.py:18
  1120.0 123.9 %all-reduce.2.cloned.1.call-start = ((), (), s32[]{:S(2)}) async-start(), calls=%async_computation.4 | async-start | bytes 262144 | tf_op jit(solution)/shard_map/while/body/eval_jaxpr/psum | solution.py:18
  1245.5 123.9 %all-reduce.2.cloned.1.call-start = ((), (), s32[]{:S(2)}) async-start(), calls=%async_computation.4 | async-start | bytes 262144 | tf_op jit(solution)/shard_map/while/body/eval_jaxpr/psum | solution.py:18
  1371.0 123.9 %all-reduce.2.cloned.1.call-start = ((), (), s32[]{:S(2)}) async-start(), calls=%async_computation.4 | async-start | bytes 262144 | tf_op jit(solution)/shard_map/while/body/eval_jaxpr/psum | solution.py:18
  1496.5 123.9 %all-reduce.2.cloned.1.call-start = ((), (), s32[]{:S(2)}) async-start(), calls=%async_computation.4 | async-start | bytes 262144 | tf_op jit(solution)/shard_map/while/body/eval_jaxpr/psum | solution.py:18
  1622.0 123.9 %all-reduce.2.cloned.1.call-start = ((), (), s32[]{:S(2)}) async-start(), calls=%async_computation.4 | async-start | bytes 262144 | tf_op jit(solution)/shard_map/while/body/eval_jaxpr/psum | solution.py:18
  1747.5 123.9 %all-reduce.2.cloned.1.call-start = ((), (), s32[]{:S(2)}) async-start(), calls=%async_computation.4 | async-start | bytes 262144 | tf_op jit(solution)/shard_map/while/body/eval_jaxpr/psum | solution.py:18
  1873.0 123.9 %all-reduce.2.cloned.1.call-start = ((), (), s32[]{:S(2)}) async-start(), calls=%async_computation.4 | async-start | bytes 262144 | tf_op jit(solution)/shard_map/while/body/eval_jaxpr/psum | solution.py:18
  1998.5 123.9 %all-reduce.2.cloned.1.call-start = ((), (), s32[]{:S(2)}) async-start(), calls=%async_computation.4 | async-start | bytes 262144 | tf_op jit(solution)/shard_map/while/body/eval_jaxpr/psum | solution.py:18
  2124.0 123.9 %all-reduce.2.cloned.1.call-start = ((), (), s32[]{:S(2)}) async-start(), calls=%async_computation.4 | async-start | bytes 262144 | tf_op jit(solution)/shard_map/while/body/eval_jaxpr/psum | solution.py:18
  (10 other events, 76.9 us)
Sparse Core Ops, SparseCore 0:
  63.7 34.9 all-gather.4
  101.8 34.2 all-gather.6
  137.8 91.5 all-gather.8
  247.0 118.4 all-reduce.1
  372.2 118.6 all-reduce.1
  497.7 118.6 all-reduce.1
  623.2 118.6 all-reduce.1
  748.7 118.6 all-reduce.1
  874.2 118.6 all-reduce.1
  999.7 118.6 all-reduce.1
  1125.2 118.6 all-reduce.1
  1250.7 118.6 all-reduce.1
  1376.2 118.6 all-reduce.1
  1501.7 118.6 all-reduce.1
  1627.2 118.6 all-reduce.1
  1752.7 118.6 all-reduce.1
  1878.1 118.6 all-reduce.1
  2003.7 118.6 all-reduce.1
  2129.2 118.6 all-reduce.1
where the time goes:
time: 2270 us
  waiting for transfers between devices  2080 us (92%)
  matrix products  126 us (6%)
  other arithmetic  34.7 us (2%)
    psum x16, waiting for transfers between devices, from_root(): return lax.psum(block, axis)  1900 us
    dot_general x17, matrix products, contract_first(): lax.dot_general(left_rows, right_rows, (((0,), (0,)), ((), ())), precisio...  84.8 us
    all_gather x1, waiting for transfers between devices, local(): lax.all_gather(memory_matrix[0], 'seg', axis=0, tiled=True)  75.3 us
    ppermute x1, waiting for transfers between devices, shifted(): lax.ppermute(shard, axis, [(i, (i + by) % size) for i in range(size)])  51.4 us
  transfers between devices with their start and end apart: 21, of which 21 were waited for; matrix products, arithmetic and copies ran while one was open for 1% of the time, Pallas kernels for 0%

commit v1 on v0

--- a/solution.py
+++ b/solution.py
@@ -91,7 +91,13 @@
     mixing = seen_cols * key_gram * (gate_rates / key_scales)[None, :]
     my_keys = lax.dynamic_slice_in_dim(key_rows, my_index * MEM, MEM, 0)
     probes = jnp.concatenate([queries, my_keys], axis=0)
-    probed_all = contract_last(probes, lax.all_gather(memory_matrix[0], "seg", axis=0, tiled=True))
+    probed_all = contract_last(
+        probes,
+        jnp.concatenate(
+            lax.all_to_all(jnp.stack([memory_matrix[0]] * lax.axis_size("seg")), "seg", 0, 0),
+            axis=0,
+        ),
+    )
     base_read = probed_all[:row_count]
     probed_keys = probed_all[row_count:]
     my_fresh = fresh_flag[my_index]

time: 2270 us -> 2380 us (1.048)
  waiting for transfers between devices: 2080 us -> 2160 us
    all_gather x1, waiting for transfers between devices: 16.4 us -> 161 us  [local(): key_rows = lax.all_gather(key_part, 'seg', axis=1, tiled=True)]
    all_gather x1 -> x0, waiting for transfers between devices: 75.3 us -> none  [local(): lax.all_gather(memory_matrix[0], 'seg', axis=0, tiled=True)]
  transfers between devices with their start and end apart: 21 -> 20, of which waited for: 21 -> 19; matrix products, arithmetic and copies ran while one was open for 1% -> 1% of each run, Pallas kernels for 0% -> 0%
where the time goes in v1:
time: 2380 us; the launch traced here: 2370 us
  waiting for transfers between devices  2160 us (91%)
  matrix products  125 us (5%)
  other arithmetic  35.1 us (1%)
    psum x16, waiting for transfers between devices, from_root(): return lax.psum(block, axis)  1910 us
    all_gather x1, waiting for transfers between devices, local(): key_rows = lax.all_gather(key_part, 'seg', axis=1, tiled=True)  161 us
    dot_general x17, matrix products, contract_first(): lax.dot_general(left_rows, right_rows, (((0,), (0,)), ((), ())), precisio...  83.3 us
    ppermute x1, waiting for transfers between devices, shifted(): lax.ppermute(shard, axis, [(i, (i + by) % size) for i in range(size)])  51.4 us
  transfers between devices with their start and end apart: 20, of which 19 were waited for; matrix products, arithmetic and copies ran while one was open for 1% of the time, Pallas kernels for 0%

profile of v1, /device:TPU:1, one launch (start us, length us, event | category | flops | bytes accessed | tf_op | source)
XLA Modules:
  0.0 2374.4 jit_solution(1279155473250602112)
XLA Ops:
  10.1 51.4 %collective-permute-done = bf16[1,1,272,4096]{3,2,1,0:T(8,128)(2,1)S(1)} collective-permute-done((bf16[1,1,272,4096]{3,2,1,0:T(8,128)(2,1)}, bf16[1,1,272,4096]{3,2,1,0:T(8,128)(2,1)S(1)}, u32[]{:S(2)}, u32[]{:S(2)}) %collective-permute-start) | collective-permute-done | bytes 2228256 | tf_op jit(solution)/shard_map/ppermute | solution.py:13
  64.1 35.1 %all-gather.3.cloned.1.call-done = bf16[256,4096]{1,0:T(8,128)(2,1)} async-done(((bf16[16,4096]{1,0:T(8,128)(2,1)}), bf16[256,4096]{1,0:T(8,128)(2,1)}) %all-gather.3.cloned.1.call-update) | async-done | bytes 2097168 | tf_op jit(solution)/shard_map/all_gather | solution.py:67
  101.6 10.3 all_to_all.14
  138.8 161.1 %all-gather.5.cloned.1.call-done = bf16[256,2048]{1,0:T(8,128)(2,1)} async-done(((bf16[256,128]{1,0:T(8,128)(2,1)}), bf16[256,2048]{1,0:T(8,128)(2,1)}) %all-gather.5.cloned.1.call-update) | async-done | bytes 1048592 | tf_op jit(solution)/shard_map/all_gather | solution.py:73
  304.2 12.3 multiply_reduce_fusion.1
  320.2 9.1 fusion.36
  332.8 2020.7 %while.13 = (s32[]{:T(128)}, f32[256,4096]{1,0:T(8,128)}, f32[256,256]{1,0:T(8,128)S(1)}, f32[16,4096]{1,0:T(8,128)S(1)}, s32[]{:T(128)}, /*index=5*/s32[]{:T(128)}, s32[]{:T(128)}, s32[]{:T(128)}, u32[]{:T(128)}, u32[]{:T(128)}) while((s32[]{:T(128)}, f32[256,4096]{1,0:T(8,128)}, f32[256,256]{1,0:T(8,128)S(1)}, f32[16,4096]{1,0:T(8,128)S(1)}, ...), condition=%wide.region_6.7_spmd, body=%wide.region_4.6_spmd.sunk | while | flops 201654288 | bytes 5898477 | solution.py:117
  337.8 132.8 %all-reduce.2.cloned.1.call-done = bf16[16,4096]{1,0:T(8,128)(2,1)} async-done(((bf16[16,4096]{1,0:T(8,128)(2,1)}), bf16[16,4096]{1,0:T(8,128)(2,1)}) %all-reduce.2.cloned.1.call-update) | async-done | bytes 131088 | tf_op jit(solution)/shard_map/while/body/eval_jaxpr/psum | solution.py:18
  477.1 118.8 %all-reduce.2.cloned.1.call-done = bf16[16,4096]{1,0:T(8,128)(2,1)} async-done(((bf16[16,4096]{1,0:T(8,128)(2,1)}), bf16[16,4096]{1,0:T(8,128)(2,1)}) %all-reduce.2.cloned.1.call-update) | async-done | bytes 131088 | tf_op jit(solution)/shard_map/while/body/eval_jaxpr/psum | solution.py:18
  602.6 118.8 %all-reduce.2.cloned.1.call-done = bf16[16,4096]{1,0:T(8,128)(2,1)} async-done(((bf16[16,4096]{1,0:T(8,128)(2,1)}), bf16[16,4096]{1,0:T(8,128)(2,1)}) %all-reduce.2.cloned.1.call-update) | async-done | bytes 131088 | tf_op jit(solution)/shard_map/while/body/eval_jaxpr/psum | solution.py:18
  728.0 118.8 %all-reduce.2.cloned.1.call-done = bf16[16,4096]{1,0:T(8,128)(2,1)} async-done(((bf16[16,4096]{1,0:T(8,128)(2,1)}), bf16[16,4096]{1,0:T(8,128)(2,1)}) %all-reduce.2.cloned.1.call-update) | async-done | bytes 131088 | tf_op jit(solution)/shard_map/while/body/eval_jaxpr/psum | solution.py:18
  853.4 118.8 %all-reduce.2.cloned.1.call-done = bf16[16,4096]{1,0:T(8,128)(2,1)} async-done(((bf16[16,4096]{1,0:T(8,128)(2,1)}), bf16[16,4096]{1,0:T(8,128)(2,1)}) %all-reduce.2.cloned.1.call-update) | async-done | bytes 131088 | tf_op jit(solution)/shard_map/while/body/eval_jaxpr/psum | solution.py:18
  978.8 118.8 %all-reduce.2.cloned.1.call-done = bf16[16,4096]{1,0:T(8,128)(2,1)} async-done(((bf16[16,4096]{1,0:T(8,128)(2,1)}), bf16[16,4096]{1,0:T(8,128)(2,1)}) %all-reduce.2.cloned.1.call-update) | async-done | bytes 131088 | tf_op jit(solution)/shard_map/while/body/eval_jaxpr/psum | solution.py:18
  1104.3 118.8 %all-reduce.2.cloned.1.call-done = bf16[16,4096]{1,0:T(8,128)(2,1)} async-done(((bf16[16,4096]{1,0:T(8,128)(2,1)}), bf16[16,4096]{1,0:T(8,128)(2,1)}) %all-reduce.2.cloned.1.call-update) | async-done | bytes 131088 | tf_op jit(solution)/shard_map/while/body/eval_jaxpr/psum | solution.py:18
  1229.7 118.8 %all-reduce.2.cloned.1.call-done = bf16[16,4096]{1,0:T(8,128)(2,1)} async-done(((bf16[16,4096]{1,0:T(8,128)(2,1)}), bf16[16,4096]{1,0:T(8,128)(2,1)}) %all-reduce.2.cloned.1.call-update) | async-done | bytes 131088 | tf_op jit(solution)/shard_map/while/body/eval_jaxpr/psum | solution.py:18
  1355.1 118.8 %all-reduce.2.cloned.1.call-done = bf16[16,4096]{1,0:T(8,128)(2,1)} async-done(((bf16[16,4096]{1,0:T(8,128)(2,1)}), bf16[16,4096]{1,0:T(8,128)(2,1)}) %all-reduce.2.cloned.1.call-update) | async-done | bytes 131088 | tf_op jit(solution)/shard_map/while/body/eval_jaxpr/psum | solution.py:18
  1480.5 118.8 %all-reduce.2.cloned.1.call-done = bf16[16,4096]{1,0:T(8,128)(2,1)} async-done(((bf16[16,4096]{1,0:T(8,128)(2,1)}), bf16[16,4096]{1,0:T(8,128)(2,1)}) %all-reduce.2.cloned.1.call-update) | async-done | bytes 131088 | tf_op jit(solution)/shard_map/while/body/eval_jaxpr/psum | solution.py:18
  1606.0 118.8 %all-reduce.2.cloned.1.call-done = bf16[16,4096]{1,0:T(8,128)(2,1)} async-done(((bf16[16,4096]{1,0:T(8,128)(2,1)}), bf16[16,4096]{1,0:T(8,128)(2,1)}) %all-reduce.2.cloned.1.call-update) | async-done | bytes 131088 | tf_op jit(solution)/shard_map/while/body/eval_jaxpr/psum | solution.py:18
  1731.4 118.8 %all-reduce.2.cloned.1.call-done = bf16[16,4096]{1,0:T(8,128)(2,1)} async-done(((bf16[16,4096]{1,0:T(8,128)(2,1)}), bf16[16,4096]{1,0:T(8,128)(2,1)}) %all-reduce.2.cloned.1.call-update) | async-done | bytes 131088 | tf_op jit(solution)/shard_map/while/body/eval_jaxpr/psum | solution.py:18
  1856.8 118.8 %all-reduce.2.cloned.1.call-done = bf16[16,4096]{1,0:T(8,128)(2,1)} async-done(((bf16[16,4096]{1,0:T(8,128)(2,1)}), bf16[16,4096]{1,0:T(8,128)(2,1)}) %all-reduce.2.cloned.1.call-update) | async-done | bytes 131088 | tf_op jit(solution)/shard_map/while/body/eval_jaxpr/psum | solution.py:18
  1982.2 118.8 %all-reduce.2.cloned.1.call-done = bf16[16,4096]{1,0:T(8,128)(2,1)} async-done(((bf16[16,4096]{1,0:T(8,128)(2,1)}), bf16[16,4096]{1,0:T(8,128)(2,1)}) %all-reduce.2.cloned.1.call-update) | async-done | bytes 131088 | tf_op jit(solution)/shard_map/while/body/eval_jaxpr/psum | solution.py:18
  2107.6 118.8 %all-reduce.2.cloned.1.call-done = bf16[16,4096]{1,0:T(8,128)(2,1)} async-done(((bf16[16,4096]{1,0:T(8,128)(2,1)}), bf16[16,4096]{1,0:T(8,128)(2,1)}) %all-reduce.2.cloned.1.call-update) | async-done | bytes 131088 | tf_op jit(solution)/shard_map/while/body/eval_jaxpr/psum | solution.py:18
  2233.1 118.8 %all-reduce.2.cloned.1.call-done = bf16[16,4096]{1,0:T(8,128)(2,1)} async-done(((bf16[16,4096]{1,0:T(8,128)(2,1)}), bf16[16,4096]{1,0:T(8,128)(2,1)}) %all-reduce.2.cloned.1.call-update) | async-done | bytes 131088 | tf_op jit(solution)/shard_map/while/body/eval_jaxpr/psum | solution.py:18
  2357.4 10.1 fusion.9
  (157 shorter events, 155.7 us)
Async XLA Ops:
  7.2 92.0 %copy-start = (bf16[1,4096,256]{2,1,0:T(8,128)(2,1)S(1)}, bf16[1,4096,256]{2,1,0:T(8,128)(2,1)}, u32[]{:S(2)}) copy-start(bf16[1,4096,256]{2,1,0:T(8,128)(2,1)} %param.14) | copy-start | bytes 6291460
  7.2 92.0 %all-gather.3.cloned.1.call-start = ((), (), s32[]{:S(2)}) async-start(), calls=%async_computation.2 | async-start | bytes 2228224 | tf_op jit(solution)/shard_map/all_gather | solution.py:67
  7.2 54.2 %collective-permute-start = (bf16[1,1,272,4096]{3,2,1,0:T(8,128)(2,1)}, bf16[1,1,272,4096]{3,2,1,0:T(8,128)(2,1)S(1)}, u32[]{:S(2)}, u32[]{:S(2)}) collective-permute-start(bf16[1,1,272,4096]{3,2,1,0:T(8,128)(2,1)} %param.11), channel_id=1, source_target_pairs={{0,1},{1,2},{2,3},{3,4},{4,5},{5,6},{6,7},{7,0},{8,9},{9,10},{10,1... | collective-permute-start | bytes 6684680 | tf_op jit(solution)/shard_map/ppermute | solution.py:13
  117.8 202.3 %all-to-all-start = ((bf16[16,256,2048]{2,1,0:T(8,128)(2,1)}), bf16[16,256,2048]{2,1,0:T(8,128)(2,1)}, u32[]{:S(2)}, u32[]{:S(2)}) async-start(bf16[16,256,2048]{2,1,0:T(8,128)(2,1)} %stack.3), calls=%async_computation | async-start | bytes 33554432 | tf_op jit(solution)/shard_map/all_to_all | solution.py:97
  123.5 176.4 %all-gather.5.cloned.1.call-start = ((), (), s32[]{:S(2)}) async-start(), calls=%async_computation.3 | async-start | bytes 1114112 | tf_op jit(solution)/shard_map/all_gather | solution.py:73
  138.7 165.2 %copy-start.16 = (f32[1,256]{1,0:T(1,128)S(1)}, f32[1,256]{1,0:T(1,128)}, u32[]{:S(2)}) copy-start(f32[1,256]{1,0:T(1,128)} %fusion.63) | copy-start | bytes 3076
  138.7 165.4 %copy-start.18 = (f32[272]{0:T(512)S(1)}, f32[272]{0:T(512)}, u32[]{:S(2)}) copy-start(f32[272]{0:T(512)} %copy-done.17) | copy-start | bytes 3268
  332.8 2020.8 %copy-start.14 = (f32[256]{0:T(256)S(1)}, f32[256]{0:T(256)}, u32[]{:S(2)}) copy-start(f32[256]{0:T(256)} %mul.175) | copy-start | bytes 3076
  332.8 137.8 %all-reduce.2.cloned.1.call-start = ((), (), s32[]{:S(2)}) async-start(), calls=%async_computation.4 | async-start | bytes 262144 | tf_op jit(solution)/shard_map/while/body/eval_jaxpr/psum | solution.py:18
  472.2 123.8 %all-reduce.2.cloned.1.call-start = ((), (), s32[]{:S(2)}) async-start(), calls=%async_computation.4 | async-start | bytes 262144 | tf_op jit(solution)/shard_map/while/body/eval_jaxpr/psum | solution.py:18
  597.6 123.8 %all-reduce.2.cloned.1.call-start = ((), (), s32[]{:S(2)}) async-start(), calls=%async_computation.4 | async-start | bytes 262144 | tf_op jit(solution)/shard_map/while/body/eval_jaxpr/psum | solution.py:18
  723.0 123.8 %all-reduce.2.cloned.1.call-start = ((), (), s32[]{:S(2)}) async-start(), calls=%async_computation.4 | async-start | bytes 262144 | tf_op jit(solution)/shard_map/while/body/eval_jaxpr/psum | solution.py:18
  848.4 123.8 %all-reduce.2.cloned.1.call-start = ((), (), s32[]{:S(2)}) async-start(), calls=%async_computation.4 | async-start | bytes 262144 | tf_op jit(solution)/shard_map/while/body/eval_jaxpr/psum | solution.py:18
  973.9 123.8 %all-reduce.2.cloned.1.call-start = ((), (), s32[]{:S(2)}) async-start(), calls=%async_computation.4 | async-start | bytes 262144 | tf_op jit(solution)/shard_map/while/body/eval_jaxpr/psum | solution.py:18
  1099.3 123.8 %all-reduce.2.cloned.1.call-start = ((), (), s32[]{:S(2)}) async-start(), calls=%async_computation.4 | async-start | bytes 262144 | tf_op jit(solution)/shard_map/while/body/eval_jaxpr/psum | solution.py:18
  1224.7 123.8 %all-reduce.2.cloned.1.call-start = ((), (), s32[]{:S(2)}) async-start(), calls=%async_computation.4 | async-start | bytes 262144 | tf_op jit(solution)/shard_map/while/body/eval_jaxpr/psum | solution.py:18
  1350.1 123.8 %all-reduce.2.cloned.1.call-start = ((), (), s32[]{:S(2)}) async-start(), calls=%async_computation.4 | async-start | bytes 262144 | tf_op jit(solution)/shard_map/while/body/eval_jaxpr/psum | solution.py:18
  1475.6 123.8 %all-reduce.2.cloned.1.call-start = ((), (), s32[]{:S(2)}) async-start(), calls=%async_computation.4 | async-start | bytes 262144 | tf_op jit(solution)/shard_map/while/body/eval_jaxpr/psum | solution.py:18
  1601.0 123.8 %all-reduce.2.cloned.1.call-start = ((), (), s32[]{:S(2)}) async-start(), calls=%async_computation.4 | async-start | bytes 262144 | tf_op jit(solution)/shard_map/while/body/eval_jaxpr/psum | solution.py:18
  1726.4 123.8 %all-reduce.2.cloned.1.call-start = ((), (), s32[]{:S(2)}) async-start(), calls=%async_computation.4 | async-start | bytes 262144 | tf_op jit(solution)/shard_map/while/body/eval_jaxpr/psum | solution.py:18
  1851.8 123.8 %all-reduce.2.cloned.1.call-start = ((), (), s32[]{:S(2)}) async-start(), calls=%async_computation.4 | async-start | bytes 262144 | tf_op jit(solution)/shard_map/while/body/eval_jaxpr/psum | solution.py:18
  1977.2 123.8 %all-reduce.2.cloned.1.call-start = ((), (), s32[]{:S(2)}) async-start(), calls=%async_computation.4 | async-start | bytes 262144 | tf_op jit(solution)/shard_map/while/body/eval_jaxpr/psum | solution.py:18
  2102.6 123.8 %all-reduce.2.cloned.1.call-start = ((), (), s32[]{:S(2)}) async-start(), calls=%async_computation.4 | async-start | bytes 262144 | tf_op jit(solution)/shard_map/while/body/eval_jaxpr/psum | solution.py:18
  2228.1 123.8 %all-reduce.2.cloned.1.call-start = ((), (), s32[]{:S(2)}) async-start(), calls=%async_computation.4 | async-start | bytes 262144 | tf_op jit(solution)/shard_map/while/body/eval_jaxpr/psum | solution.py:18
  (16 other events, 91.8 us)
Sparse Core Ops, SparseCore 0:
  64.2 34.9 all-gather.2
  126.3 173.5 all-gather.4
  337.9 132.5 all-reduce.1
  477.3 118.6 all-reduce.1
  602.7 118.6 all-reduce.1
  728.1 118.6 all-reduce.1
  853.5 118.6 all-reduce.1
  979.0 118.6 all-reduce.1
  1104.4 118.6 all-reduce.1
  1229.8 118.6 all-reduce.1
  1355.2 118.6 all-reduce.1
  1480.7 118.6 all-reduce.1
  1606.1 118.6 all-reduce.1
  1731.5 118.6 all-reduce.1
  1856.9 118.6 all-reduce.1
  1982.3 118.6 all-reduce.1
  2107.8 118.6 all-reduce.1
  2233.2 118.6 all-reduce.1
